TPU v7x, 256 devices: a whole 4x4x8 slice. The times are simulated.
256 devices in a mesh: shell: 8 (over z), sector: 32 (over x, y, core).
Axes of the slice: x: 4, y: 4, z: 8, core: 2. Of those that a mesh axis runs over, the one named last changes fastest.
Arguments:
- bricks: bfloat16 [8, 256, 32, 512], P('shell', 'sector'), may hold values from -6 to 6
- conv_w: bfloat16 [32, 864], replicated, may hold values from -0.21875 to 0.21875
- conv_b: float32 [32], replicated, may hold values from -3 to 3
- head_w1: bfloat16 [32, 64], replicated, may hold values from -1 to 1
- head_b1: float32 [64], replicated, may hold values from -3 to 3
- head_w2: float32 [64, 2], replicated, may hold values from -0.75 to 0.75
- queries: int32 [8, 1024, 256], P('shell', 'sector'), may hold values from -1 to 4095, as said below
- sample_src: int32 [8, 131072], P('shell', 'sector'), may hold values from 0 to 8191, as said below
- depth_target: float32 [16384], P('sector'), may hold values from 0.1 to 0.9
- inten_target: float32 [16384], P('sector'), may hold values from 0 to 1
- drop_label: int32 [16384], P('sector'), may hold values 0 or 1
Outputs:
- loss_mean: float32 [], replicated
- grad_conv_w: float32 [32, 864], replicated
- grad_conv_b: float32 [32], replicated
- grad_head_w1: float32 [32, 64], replicated
- grad_head_b1: float32 [64], replicated
- grad_head_w2: float32 [64, 2], replicated
- grad_bricks: bfloat16 [8, 256, 32, 512], P('shell', 'sector')
- ray_depth: float32 [16384], P('sector')
Inputs may be any that keep to these rules, and one draw needn't show every extreme that they name: `queries`: entry of the buffer from a device of sector v to owner w: a cell address (brick of the owner times 512 plus cell) or -1 for an empty slot. Every sample of a device holds exactly one live slot, named by sample_src as w * 256 + slot. In every shell one owner receives full buffers of 256 from every sector. `sample_src`: A slot w * 256 + slot of the sample's own device; distinct samples of a device have distinct slots.
All inputs are finite; a program needn't handle non-finite values. No bound on the sum of `drop_label` on one device may be relied on, other than what follows from the above.
Results may differ from a plain program's by a relative error of at most 0.0015.
The roundings to bfloat16 on the way count: a program that leaves them out, or rounds other values in their place, can miss the bound.
Values may be sent and summed in bfloat16 or wider, within the bound.
No kernel may reach another device: no remote copies, remote signals or barrier semaphores. Data moves between devices by JAX's collectives and lax.ppermute only.
A program may use at most 192 MiB of HBM per device.

v0:
```python
import math
import jax
import jax.numpy as jnp
from jax import lax
from jax.sharding import PartitionSpec as P

SAMP = 8
HIGHEST = lax.Precision.HIGHEST
CUBE_OFFSETS = [(a, b, c) for a in range(3) for b in range(3) for c in range(3)]


def entering(value, axis, join, neutral, backward):
    count, mine = (lax.axis_size(axis), lax.axis_index(axis))
    pieces = lax.all_gather(value, axis)
    if backward:
        pieces = pieces[::-1]
        mine = count - 1 - mine
    total = jnp.full_like(value, 0) + jnp.asarray(neutral, value.dtype)

    def hop(position, total):
        longer = join(total, pieces[position])
        return jnp.where(position < mine, longer, total)

    return lax.fori_loop(0, count - 1, hop, total)


def unfold_cells(block_set):
    brick_count = block_set.shape[0]
    channel_width = block_set.shape[1]
    cube = block_set.reshape(brick_count, channel_width, 8, 8, 8)
    padded = jnp.pad(cube, ((0, 0), (0, 0), (1, 1), (1, 1), (1, 1)))
    columns = [
        padded[:, :, a : a + 8, b : b + 8, c : c + 8].reshape(brick_count, channel_width, 512)
        for a, b, c in CUBE_OFFSETS
    ]
    return jnp.stack(columns, axis=1).reshape(brick_count, 27 * channel_width, 512)


def conv_backward(block_set, block_cot, conv_w, conv_b):
    unfolded = unfold_cells(block_set)
    pre_act = (
        jnp.einsum("oc,bcn->obn", conv_w, unfolded, preferred_element_type=jnp.float32)
        + conv_b[:, None, None]
    )
    _, gelu_pull = jax.vjp(jax.nn.gelu, pre_act)
    pre_grad = gelu_pull(block_cot)[0].astype(jnp.bfloat16)
    weight_grad = jnp.einsum("obn,bcn->oc", pre_grad, unfolded, preferred_element_type=jnp.float32)
    bias_grad = jnp.sum(pre_grad.astype(jnp.float32), axis=(1, 2))
    column_grad = jnp.einsum("oc,obn->bcn", conv_w, pre_grad, preferred_element_type=jnp.float32)
    _, fold_pull = jax.vjp(unfold_cells, jnp.zeros(block_set.shape, jnp.float32))
    block_grad = fold_pull(column_grad)[0]
    return (weight_grad, bias_grad, block_grad.astype(jnp.bfloat16))


def field_head(feature_cols, weight_one, bias_one, weight_two):
    hidden = (
        jnp.einsum("ch,cm->hm", weight_one, feature_cols, precision=HIGHEST) + bias_one[:, None]
    )
    outputs = jnp.einsum("hk,hm->km", weight_two, jax.nn.gelu(hidden), precision=HIGHEST)
    return (jax.nn.softplus(outputs[0]), jax.nn.sigmoid(outputs[1]))


def render_terms(density, intensity, depth_grid, step_size):
    optical = density * step_size
    before = jnp.cumsum(optical, axis=-1) - optical
    weights = jnp.exp(-before) * (1.0 - jnp.exp(-optical))
    return (
        jnp.sum(weights * depth_grid, axis=-1),
        jnp.sum(weights * intensity, axis=-1),
        jnp.sum(optical, axis=-1),
    )


def add_terms(first_term, second_term):
    return first_term + second_term


def local(
    bricks,
    conv_w,
    conv_b,
    head_w1,
    head_b1,
    head_w2,
    queries,
    sample_src,
    depth_target,
    inten_target,
    drop_label,
):
    shells = lax.axis_size("shell")
    sectors = lax.axis_size("sector")
    shell_index = lax.axis_index("shell")
    local_bricks = bricks[0]
    brick_count = local_bricks.shape[0]
    channels = local_bricks.shape[1]
    group_size = math.gcd(brick_count, 8)
    group_cols = group_size * 512
    group_total = brick_count // group_size
    weight_one = head_w1.astype(jnp.float32)
    brick_groups = local_bricks.reshape(group_total, group_size, channels, 512)

    def decode_group(group_id, table_now):
        block_set = lax.dynamic_index_in_dim(brick_groups, group_id, 0, keepdims=False)
        pre_act = (
            jnp.einsum(
                "oc,bcn->obn", conv_w, unfold_cells(block_set), preferred_element_type=jnp.float32
            )
            + conv_b[:, None, None]
        )
        values = jax.nn.gelu(pre_act).astype(jnp.bfloat16).reshape(channels, group_cols)
        return values

    cell_table = lax.fori_loop(
        0, group_total, decode_group, jnp.zeros((channels, brick_count * 512), jnp.bfloat16)
    )
    requests = queries[0]
    capacity = requests.shape[1]
    owner_addr = lax.all_to_all(
        requests, "sector", split_axis=0, concat_axis=0, tiled=True
    ).reshape(-1)
    live_slot = owner_addr >= 0
    picked = jnp.take(cell_table, jnp.where(live_slot, owner_addr, 0), axis=1)
    owner_feats = jnp.where(live_slot[None, :], picked, jnp.zeros((), jnp.bfloat16))
    sources = sample_src[0]
    replies = lax.all_to_all(
        owner_feats.reshape(channels, sectors, capacity),
        "sector",
        split_axis=1,
        concat_axis=1,
        tiled=True,
    )
    sample_cols = jnp.take(replies.reshape(channels, sectors * capacity), sources, axis=1).astype(
        jnp.float32
    )
    (density, intensity), head_pull = jax.vjp(field_head, sample_cols, weight_one, head_b1, head_w2)
    ray_count = sources.shape[0] // SAMP
    density = density.reshape(ray_count, SAMP)
    intensity = intensity.reshape(ray_count, SAMP)
    step_size = 2.0 / (shells * SAMP)
    depth_grid = (
        shell_index.astype(jnp.float32) * SAMP + jnp.arange(SAMP, dtype=jnp.float32) + 0.5
    ) / (shells * SAMP)

    def local_render(dens_in, inten_in):
        return render_terms(dens_in, inten_in, depth_grid, step_size)

    (shell_depth, shell_inten, shell_tau), render_pull = jax.vjp(local_render, density, intensity)
    dropped = drop_label.astype(jnp.float32)
    kept_weight = 1.0 - dropped
    zeros_rays = jnp.zeros_like(shell_tau)
    prefix = entering(shell_tau, "shell", add_terms, zeros_rays, False)
    entry_trans = jnp.exp(-prefix)
    ray_depth, ray_inten, tau_total = lax.psum(
        (entry_trans * shell_depth, entry_trans * shell_inten, shell_tau), "shell"
    )
    escape = jnp.exp(-tau_total)
    grad_depth = 2.0 * kept_weight * (ray_depth - depth_target)
    grad_inten = 2.0 * kept_weight * (ray_inten - inten_target)
    own_weight = (grad_depth * shell_depth + grad_inten * shell_inten) * entry_trans
    behind = entering(own_weight, "shell", add_terms, zeros_rays, True)
    grad_escape = 2.0 * (escape - dropped)
    dens_grad, inten_grad = render_pull(
        (grad_depth * entry_trans, grad_inten * entry_trans, -grad_escape * escape - behind)
    )
    ray_loss = jnp.sum(
        kept_weight * ((ray_depth - depth_target) ** 2 + (ray_inten - inten_target) ** 2)
        + (escape - dropped) ** 2
    )
    loss_mean = lax.psum(ray_loss, "sector") / (ray_count * sectors)
    sample_grad, grad_one, grad_bias_one, grad_two = head_pull(
        (dens_grad.reshape(-1), inten_grad.reshape(-1))
    )
    buckets = jnp.zeros((channels, sectors * capacity), jnp.float32).at[:, sources].set(sample_grad)
    owner_grad = lax.all_to_all(
        buckets.reshape(channels, sectors, capacity),
        "sector",
        split_axis=1,
        concat_axis=1,
        tiled=True,
    ).reshape(channels, sectors * capacity)
    target_index = jnp.where(live_slot, owner_addr, brick_count * 512)
    table_grad = (
        jnp.zeros((channels, brick_count * 512), jnp.float32)
        .at[:, target_index]
        .add(owner_grad, mode="drop")
    )

    def conv_back(totals, group_id):
        block_set = lax.dynamic_index_in_dim(brick_groups, group_id, 0, keepdims=False)
        block_cot = table_grad.reshape(channels, group_size, 512)
        weight_grad, bias_grad, block_grad = conv_backward(block_set, block_cot, conv_w, conv_b)
        return ((totals[0] + weight_grad, totals[1] + bias_grad), block_grad)

    start = (jnp.zeros(conv_w.shape, jnp.float32), jnp.zeros_like(conv_b))
    (conv_grad, conv_bias_grad), brick_grads = lax.scan(
        conv_back, start, jnp.arange(group_total, dtype=jnp.int32)
    )
    summed = lax.psum(
        (conv_grad, conv_bias_grad, grad_one, grad_bias_one, grad_two), ("shell", "sector")
    )
    return (
        loss_mean,
        summed[0],
        summed[1],
        summed[2],
        summed[3],
        summed[4],
        brick_grads,
        ray_depth,
    )


def solution(mesh):
    return jax.shard_map(
        local,
        mesh=mesh,
        in_specs=(
            P("shell", "sector", None, None),
            P(),
            P(),
            P(),
            P(),
            P(),
            P("shell", "sector", None),
            P("shell", "sector"),
            P("sector"),
            P("sector"),
            P("sector"),
        ),
        out_specs=(P(), P(), P(), P(), P(), P(), P("shell", "sector", None, None), P("sector")),
        check_vma=False,
    )
```

profile of v0, /device:TPU:1, one launch (start us, length us, event | category | flops | bytes accessed | tf_op | source)
XLA Modules:
  0.0 665.0 jit_solution(13087959850178110753)
XLA Ops:
  8.6 8.6 %all-to-all-start = ((s32[32,1,256]{2,1,0:T(1,128)}), s32[32,1,256]{2,1,0:T(1,128)S(1)}, u32[]{:S(2)}, u32[]{:S(2)}) async-start(s32[32,1,256]{2,1,0:T(1,128)} %all_to_all.12), calls=%async_computation | async-start | bytes 65536 | tf_op jit(solution)/shard_map/all_to_all | solution.py:119
  18.6 3.4 pad_slice_fusion.1
  22.1 6.8 %pad_slice_fusion = (bf16[8,32,8,8,8]{1,4,3,2,0:T(8,128)(2,1)}, bf16[8,32,8,8,8]{1,4,3,2,0:T(8,128)(2,1)}, bf16[8,32,8,8,8]{1,4,3,2,0:T(8,128)(2,1)}, bf16[8,32,...) fusion(bf16[8,32,8,8,8]{1,4,3,2,0:T(8,128)(2,1)S(1)} %bitcast.139), kind=kLoop, calls=%fused_computation.8 | loop fusion | bytes 5242880 | tf_op jit(solution)/shard_map/while/body/eval_jaxpr/slice | solution.py:33
  118.1 5.1 multiply_convert_fusion
  124.4 24.0 %gather_fusion = bf16[8192,32]{1,0:T(8,128)(2,1)S(1)} fusion(bf16[32,4096]{0,1:T(8,128)(2,1)S(1)} %bitcast.136, s32[8192]{0:T(1024)S(1)} %broadcast_clamp_fusion), kind=kCustom, calls=%fused_computation | custom fusion | bytes 1081344 | tf_op jit(solution)/shard_map/jit(_take)/gather | solution.py:123
  150.3 7.4 %all-to-all-start.1 = ((bf16[32,32,256]{2,0,1:T(8,128)(2,1)}), bf16[32,32,256]{2,0,1:T(8,128)(2,1)S(1)}, u32[]{:S(2)}, u32[]{:S(2)}) async-start(bf16[32,32,256]{2,0,1:T(8,128)(2,1)} %select_select_fusion), calls=%async_computation.1 | async-start | bytes 1048576 | tf_op jit(solution)/shard_map/all_to_all | solution.py:126
  157.8 11.5 %all-to-all-done.1 = bf16[32,32,256]{2,0,1:T(8,128)(2,1)S(1)} async-done(((bf16[32,32,256]{2,0,1:T(8,128)(2,1)}), bf16[32,32,256]{2,0,1:T(8,128)(2,1)S(1)}, u32[]{:S(2)}, u32[]{:S(2)}) %all-to-all-start.1) | async-done | bytes 524320 | tf_op jit(solution)/shard_map/all_to_all | solution.py:126
  170.4 12.1 %gather_fusion.1 = bf16[4096,32]{1,0:T(8,128)(2,1)S(1)} fusion(bf16[32,8192]{0,1:T(8,128)(2,1)S(1)} %bitcast.163, s32[4096]{0:T(1024)S(1)} %broadcast_clamp_fusion.1), kind=kCustom, calls=%fused_computation.1 | custom fusion | bytes 540672 | tf_op jit(solution)/shard_map/jit(_take)/gather | solution.py:133
  187.0 19.6 %all-gather.2 = f32[8,1,512]{2,1,0:T(1,128)S(1)} all-gather(f32[1,1,512]{2,1,0:T(1,128)S(1)} %bitcast.209), channel_id=2, replica_groups=mesh['shell'=8,'sector'=32] {'shell'}, dimensions={0}, use_global_device_ids=true | all-gather | bytes 18432 | tf_op jit(solution)/shard_map/all_gather | solution.py:14
  207.0 11.4 %all-reduce.31 = (f32[512]{0:T(512)S(1)}, f32[512]{0:T(512)S(1)}, f32[512]{0:T(512)S(1)}) all-reduce(f32[512]{0:T(512)S(1)} %get-tuple-element.265, f32[512]{0:T(512)S(1)} %get-tuple-element.360, f32[512]{0:T(512)S(1)} %get-tuple-element.359), channel_id=1, replica_groups=mesh['shell'=8,'sector'=32] {'shell'}, use_global_device_ids=true, to_apply=%region_8.9 | all-reduce | flops 1536 | bytes 12288 | tf_op jit(solution)/shard_map/psum | solution.py:154
  220.8 15.9 %all-gather.3 = f32[8,1,512]{2,1,0:T(1,128)S(1)} all-gather(f32[1,1,512]{2,1,0:T(1,128)} %bitcast.210), channel_id=3, replica_groups=mesh['shell'=8,'sector'=32] {'shell'}, dimensions={0}, use_global_device_ids=true | all-gather | bytes 18432 | tf_op jit(solution)/shard_map/all_gather | solution.py:14
  242.3 3.9 fusion.57
  246.2 13.2 %scatter_custom_fusion = f32[32,8192]{0,1:T(8,128)} fusion(s32[4096]{0:T(1024)S(1)} %bitcast.205, f32[4096,32]{1,0:T(8,128)} %fusion.57, f32[]{:T(128)} %constant.164.clone.1), kind=kCustom, calls=%fused_computation.45 | custom fusion | bytes 1049088 | tf_op jit(solution)/shard_map/scatter | solution.py:174
  259.5 3.6 copy.154
  263.1 18.7 %all-to-all-start.2 = ((f32[32,32,256]{2,0,1:T(8,128)}), f32[32,32,256]{2,0,1:T(8,128)S(1)}, u32[]{:S(2)}, u32[]{:S(2)}) async-start(f32[32,32,256]{2,0,1:T(8,128)} %copy.154), calls=%async_computation.2 | async-start | bytes 2097152 | tf_op jit(solution)/shard_map/all_to_all | solution.py:175
  281.8 71.8 %psum.66 = f32[]{:T(128)} all-reduce(f32[]{:T(128)} %get-tuple-element.354), channel_id=1, replica_groups=mesh['shell'=8,'sector'=32] {'sector'}, use_global_device_ids=true, to_apply=%region_10.11 | all-reduce | flops 1 | bytes 8 | tf_op jit(solution)/shard_map/psum | solution.py:170
  361.1 45.0 %scatter_custom_fusion.1 = f32[32,4096]{0,1:T(8,128)S(1)} fusion(s32[8192]{0:T(1024)} %bitcast.208, f32[8192,32]{1,0:T(8,128)} %copy.156, f32[]{:T(128)} %constant.164.clone.1), kind=kCustom, calls=%fused_computation.58 | custom fusion | flops 262144 | bytes 524800 | tf_op jit(solution)/shard_map/scatter-add | solution.py:186
  407.2 5.8 convolution_bitcast_fusion.2
  417.1 3.4 fusion.54
  472.8 3.0 copy.213
  490.8 3.2 copy.207
  497.9 16.8 %pad_add_fusion = f32[8,32,10,10,10]{1,4,3,2,0:T(8,128)S(1)} fusion(f32[8,32,8,8,8]{1,4,3,2,0:T(8,128)} %bitcast.148, f32[8,32,8,8,8]{1,4,3,2,0:T(8,128)} %bitcast.149, f32[8,32,8,8,8]{1,4,3,2,0:T(8,128)} %bitcast.150, f32[8,32,8,8,8]{1,4,3,2,0:T(8,128)} %bitcast.151, f32[8,32,8,8,8]{1,4,3,2,0:T(8,128)} %bitcast.152, f32[8,32,8,8,8]{1,4,3,2,0:T(8,128)} %bitcast.153, ...), kind=kLoop, calls=%fused_computation.34 | loop fusion | flops 5376000 | bytes 12558336 | tf_op jit(solution)/shard_map/while/body/eval_jaxpr/transpose(jvp())/add_any | solution.py:33
  515.8 72.8 %all-reduce.30 = (f32[32]{0:T(128)}, f32[32,64]{1,0:T(8,128)}, f32[64]{0:T(128)}, f32[64,2]{0,1:T(2,128)}) all-reduce(f32[32]{0:T(128)S(1)} %get-tuple-element.289, f32[32,64]{1,0:T(8,128)S(1)} %fusion.21, f32[64]{0:T(128)S(1)} %get-tuple-element.363, f32[64,2]{0,1:T(2,128)S(1)} %fusion.20), channel_id=1, replica_groups=mesh['shell'=8,'sector'=32] {'shell','sector'}, use_global_device_ids=true, to_apply=%region_18.19 | all-reduce | flops 2272 | bytes 18176 | tf_op jit(solution)/shard_map/psum | solution.py:199
  589.7 65.3 %all-reduce.34.cloned.1.call-done = f32[32,864]{1,0:T(8,128)} async-done(((f32[32,864]{1,0:T(8,128)}), f32[32,864]{1,0:T(8,128)}) %all-reduce.34.cloned.1.call-update) | async-done | bytes 110608 | tf_op jit(solution)/shard_map/psum | solution.py:199
  (224 shorter events, 196.0 us)
Async XLA Ops:
  7.2 110.9 %copy-start = (bf16[32,864]{1,0:T(8,128)(2,1)S(1)}, bf16[32,864]{1,0:T(8,128)(2,1)}, u32[]{:S(2)}) copy-start(bf16[32,864]{1,0:T(8,128)(2,1)} %param.16) | copy-start | bytes 165892
  8.6 115.1 %all-to-all-start = ((s32[32,1,256]{2,1,0:T(1,128)}), s32[32,1,256]{2,1,0:T(1,128)S(1)}, u32[]{:S(2)}, u32[]{:S(2)}) async-start(s32[32,1,256]{2,1,0:T(1,128)} %all_to_all.12), calls=%async_computation | async-start | bytes 65536 | tf_op jit(solution)/shard_map/all_to_all | solution.py:119
  43.6 22.6 %copy-start.8 = (bf16[8,32,8,8,8]{1,4,3,2,0:T(8,128)(2,1)S(1)}, bf16[8,32,8,8,8]{1,4,3,2,0:T(8,128)(2,1)}, u32[]{:S(2)}) copy-start(bf16[8,32,8,8,8]{1,4,3,2,0:T(8,128)(2,1)} %get-tuple-element.330) | copy-start | bytes 786436
  61.7 30.3 %copy-start.12 = (bf16[1,8,32,512]{3,2,1,0:T(8,128)(2,1)S(1)}, bf16[1,8,32,512]{3,2,1,0:T(8,128)(2,1)}, u32[]{:S(2)}) copy-start(bf16[1,8,32,512]{3,2,1,0:T(8,128)(2,1)} %param.15) | copy-start | bytes 786436
  67.2 32.2 %copy-start.7 = (bf16[8,32,8,8,8]{1,4,3,2,0:T(8,128)(2,1)S(1)}, bf16[8,32,8,8,8]{1,4,3,2,0:T(8,128)(2,1)}, u32[]{:S(2)}) copy-start(bf16[8,32,8,8,8]{1,4,3,2,0:T(8,128)(2,1)} %get-tuple-element.336) | copy-start | bytes 786436
  92.7 23.9 %copy-start.13 = (bf16[8,1,32,512]{3,2,1,0:T(8,128)(2,1)S(1)}, bf16[8,1,32,512]{3,2,1,0:T(8,128)(2,1)}, u32[]{:S(2)}) copy-start(bf16[8,1,32,512]{3,2,1,0:T(8,128)(2,1)} %copy.147) | copy-start | bytes 786436
  95.0 23.1 %copy-start.27 = (f32[32]{0:T(128)S(1)}, f32[32]{0:T(128)}, u32[]{:S(2)}) copy-start(f32[32]{0:T(128)} %param.17) | copy-start | bytes 388
  100.5 16.8 %copy-start.16 = (bf16[8,1,32,512]{3,2,1,0:T(8,128)(2,1)S(1)}, bf16[8,1,32,512]{3,2,1,0:T(8,128)(2,1)}, u32[]{:S(2)}) copy-start(bf16[8,1,32,512]{3,2,1,0:T(8,128)(2,1)} %copy.148) | copy-start | bytes 786436
  124.4 58.2 %copy-start.19 = (bf16[32,64]{1,0:T(8,128)(2,1)S(1)}, bf16[32,64]{1,0:T(8,128)(2,1)}, u32[]{:S(2)}) copy-start(bf16[32,64]{1,0:T(8,128)(2,1)} %param.18) | copy-start | bytes 12292
  124.4 58.2 %copy-start.28 = (f32[64]{0:T(128)S(1)}, f32[64]{0:T(128)}, u32[]{:S(2)}) copy-start(f32[64]{0:T(128)} %param.19) | copy-start | bytes 772
  148.4 35.0 %copy-start.29 = (f32[64,2]{0,1:T(2,128)S(1)}, f32[64,2]{0,1:T(2,128)}, u32[]{:S(2)}) copy-start(f32[64,2]{0,1:T(2,128)} %param.20) | copy-start | bytes 1540
  150.3 19.0 %all-to-all-start.1 = ((bf16[32,32,256]{2,0,1:T(8,128)(2,1)}), bf16[32,32,256]{2,0,1:T(8,128)(2,1)S(1)}, u32[]{:S(2)}, u32[]{:S(2)}) async-start(bf16[32,32,256]{2,0,1:T(8,128)(2,1)} %select_select_fusion), calls=%async_computation.1 | async-start | bytes 1048576 | tf_op jit(solution)/shard_map/all_to_all | solution.py:126
  157.7 48.9 %copy-start.26 = (f32[8]{0:T(128)}, f32[8]{0:T(128)S(1)}, u32[]{:S(2)}) copy-start(f32[8]{0:T(128)S(1)} %add_multiply_fusion.1) | copy-start | bytes 100
  157.8 60.7 %copy-start.21 = (s32[512]{0:T(512)S(1)}, s32[512]{0:T(512)}, u32[]{:S(2)}) copy-start(s32[512]{0:T(512)} %param.25) | copy-start | bytes 6148
  157.8 60.7 %copy-start.23 = (f32[512]{0:T(512)S(1)}, f32[512]{0:T(512)}, u32[]{:S(2)}) copy-start(f32[512]{0:T(512)} %param.24) | copy-start | bytes 6148
  157.8 60.7 %copy-start.24 = (f32[512]{0:T(512)S(1)}, f32[512]{0:T(512)}, u32[]{:S(2)}) copy-start(f32[512]{0:T(512)} %param.23) | copy-start | bytes 6148
  183.4 58.9 %copy-start.11 = (f32[64,4096]{1,0:T(8,128)}, f32[64,4096]{1,0:T(8,128)S(1)}, u32[]{:S(2)}) copy-start(f32[64,4096]{1,0:T(8,128)S(1)} %fusion) | copy-start | bytes 3145732
  263.1 95.2 %all-to-all-start.2 = ((f32[32,32,256]{2,0,1:T(8,128)}), f32[32,32,256]{2,0,1:T(8,128)S(1)}, u32[]{:S(2)}, u32[]{:S(2)}) async-start(f32[32,32,256]{2,0,1:T(8,128)} %copy.154), calls=%async_computation.2 | async-start | bytes 2097152 | tf_op jit(solution)/shard_map/all_to_all | solution.py:175
  281.7 373.3 %all-reduce.34.cloned.1.call-start = ((), (), s32[]{:S(2)}) async-start(), calls=%async_computation.3 | async-start | bytes 229376 | tf_op jit(solution)/shard_map/psum | solution.py:199
  358.2 48.5 %copy-start.10 = (f32[32,8,512]{2,0,1:T(8,128)S(1)}, f32[32,8,512]{2,0,1:T(8,128)}, u32[]{:S(2)}) copy-start(f32[32,8,512]{2,0,1:T(8,128)} %get-tuple-element.362) | copy-start | bytes 1572868
  497.9 16.8 %copy-start.4 = (f32[8,1,32,512]{2,3,0,1:T(8,128)S(1)}, f32[8,1,32,512]{2,3,0,1:T(8,128)}, u32[]{:S(2)}) copy-start(f32[8,1,32,512]{2,3,0,1:T(8,128)} %copy.221) | copy-start | bytes 1572868
  497.9 16.8 %copy-start.5 = (f32[8,1,32,512]{2,3,0,1:T(8,128)S(1)}, f32[8,1,32,512]{2,3,0,1:T(8,128)}, u32[]{:S(2)}) copy-start(f32[8,1,32,512]{2,3,0,1:T(8,128)} %copy.220) | copy-start | bytes 1572868
  497.9 16.8 %copy-start.6 = (f32[8,1,32,512]{2,3,0,1:T(8,128)S(1)}, f32[8,1,32,512]{2,3,0,1:T(8,128)}, u32[]{:S(2)}) copy-start(f32[8,1,32,512]{2,3,0,1:T(8,128)} %copy.219) | copy-start | bytes 1572868
  514.7 141.9 %copy-start.1 = (bf16[32,864]{1,0:T(8,128)(2,1)S(1)}, bf16[32,864]{1,0:T(8,128)(2,1)}, u32[]{:S(2)}) copy-start(bf16[32,864]{1,0:T(8,128)(2,1)} %param.16) | copy-start | bytes 165892
  (10 other events, 101.3 us)
Sparse Core Ops, SparseCore 0:
  420.6 234.3 all-reduce.33
where the time goes:
time: 677 us; the launch traced here: 665 us
  local copies, waits for them, and re-layouts  249 us (37%)
  blocking collectives  192 us (28%)
  waiting for transfers between devices  76.9 us (11%)
  other arithmetic  70.1 us (10%)
  starting transfers between devices  34.7 us (5%)
  matrix products  25.1 us (4%)
  between operations  16.9 us (2%)
    unnamed x118, local copies, waits for them, and re-layouts  119 us
    psum x1, blocking collectives, local(): lax.psum((conv_grad, conv_bias_grad, grad_one, grad_bias_one, grad_two),...  72.8 us
    psum x1, blocking collectives, local(): loss_mean = lax.psum(ray_loss, 'sector') / (ray_count * sectors)  71.8 us
    psum x1, waiting for transfers between devices, local(): lax.psum((conv_grad, conv_bias_grad, grad_one, grad_bias_one, grad_two),...  65.3 us
    reshape x26, local copies, waits for them, and re-layouts, unfold_cells(): jnp.stack(columns, axis=1).reshape(brick_count, 27 * channel_width, 512)  51.4 us
    scatter-add x1, other arithmetic, local(): table_grad = jnp.zeros((channels, brick_count * 512), jnp.float32).at[:,...  45 us
    all_gather x2, blocking collectives, entering(): pieces = lax.all_gather(value, axis)  35.5 us
    gather x2, local copies, waits for them, and re-layouts, local(): picked = jnp.take(cell_table, jnp.where(live_slot, owner_addr, 0), axis=1)  25 us
  transfers between devices with their start and end apart: 4, of which 2 were waited for; matrix products, arithmetic and copies ran while one was open for 31% of the time, Pallas kernels for 0%

commit v1 on v0

--- a/solution.py
+++ b/solution.py
@@ -196,9 +196,9 @@
     (conv_grad, conv_bias_grad), brick_grads = lax.scan(
         conv_back, start, jnp.arange(group_total, dtype=jnp.int32)
     )
-    summed = lax.psum(
-        (conv_grad, conv_bias_grad, grad_one, grad_bias_one, grad_two), ("shell", "sector")
-    )
+    summed = (conv_grad, conv_bias_grad, grad_one, grad_bias_one, grad_two)
+    for over in ("shell", "sector"):
+        summed = lax.psum(summed, over)
     return (
         loss_mean,
         summed[0],

time: 677 us -> 633 us (0.935)
  the two profiles are of different devices: /device:TPU:1 before, /device:TPU:0 now
where the time goes in v1:
time: 633 us; the launch traced here: 621 us
  local copies, waits for them, and re-layouts  248 us (39%)
  blocking collectives  213 us (34%)
  other arithmetic  75.5 us (12%)
  matrix products  25.1 us (4%)
  waiting for transfers between devices  23.9 us (4%)
  starting transfers between devices  17.6 us (3%)
  between operations  16.8 us (3%)
    psum x1, blocking collectives, local(): loss_mean = lax.psum(ray_loss, 'sector') / (ray_count * sectors)  124 us
    unnamed x108, local copies, waits for them, and re-layouts  117 us
    reshape x26, local copies, waits for them, and re-layouts, unfold_cells(): jnp.stack(columns, axis=1).reshape(brick_count, 27 * channel_width, 512)  51.4 us
    all_gather x2, blocking collectives, entering(): pieces = lax.all_gather(value, axis)  46.4 us
    scatter-add x1, other arithmetic, local(): table_grad = jnp.zeros((channels, brick_count * 512), jnp.float32).at[:,...  44.8 us
    psum x1, blocking collectives, local(): summed = lax.psum(summed, over)  27.7 us
    gather x2, local copies, waits for them, and re-layouts, local(): picked = jnp.take(cell_table, jnp.where(live_slot, owner_addr, 0), axis=1)  25 us
    add_any x1, other arithmetic, unfold_cells(): padded[:, :, a:a + 8, b:b + 8, c:c + 8]  18.2 us
  transfers between devices with their start and end apart: 5, of which 2 were waited for; matrix products, arithmetic and copies ran while one was open for 34% of the time, Pallas kernels for 0%

profile of v1, /device:TPU:0, one launch (start us, length us, event | category | flops | bytes accessed | tf_op | source)
XLA Modules:
  0.0 620.9 jit_solution(1811926216476882610)
XLA Ops:
  8.6 5.6 all-to-all-start
  15.6 3.4 pad_slice_fusion.1
  19.0 6.8 %pad_slice_fusion = (bf16[8,32,8,8,8]{1,4,3,2,0:T(8,128)(2,1)}, bf16[8,32,8,8,8]{1,4,3,2,0:T(8,128)(2,1)}, bf16[8,32,8,8,8]{1,4,3,2,0:T(8,128)(2,1)}, bf16[8,32,...) fusion(bf16[8,32,8,8,8]{1,4,3,2,0:T(8,128)(2,1)S(1)} %bitcast.139), kind=kLoop, calls=%fused_computation.8 | loop fusion | bytes 5242880 | tf_op jit(solution)/shard_map/while/body/eval_jaxpr/slice | solution.py:33
  115.1 5.1 multiply_convert_fusion
  121.4 24.0 %gather_fusion = bf16[8192,32]{1,0:T(8,128)(2,1)S(1)} fusion(bf16[32,4096]{0,1:T(8,128)(2,1)S(1)} %bitcast.136, s32[8192]{0:T(1024)S(1)} %broadcast_clamp_fusion), kind=kCustom, calls=%fused_computation | custom fusion | bytes 1081344 | tf_op jit(solution)/shard_map/jit(_take)/gather | solution.py:123
  147.4 7.4 %all-to-all-start.1 = ((bf16[32,32,256]{2,0,1:T(8,128)(2,1)}), bf16[32,32,256]{2,0,1:T(8,128)(2,1)S(1)}, u32[]{:S(2)}, u32[]{:S(2)}) async-start(bf16[32,32,256]{2,0,1:T(8,128)(2,1)} %select_select_fusion), calls=%async_computation.1 | async-start | bytes 1048576 | tf_op jit(solution)/shard_map/all_to_all | solution.py:126
  154.9 11.1 %all-to-all-done.1 = bf16[32,32,256]{2,0,1:T(8,128)(2,1)S(1)} async-done(((bf16[32,32,256]{2,0,1:T(8,128)(2,1)}), bf16[32,32,256]{2,0,1:T(8,128)(2,1)S(1)}, u32[]{:S(2)}, u32[]{:S(2)}) %all-to-all-start.1) | async-done | bytes 524320 | tf_op jit(solution)/shard_map/all_to_all | solution.py:126
  167.0 12.1 %gather_fusion.1 = bf16[4096,32]{1,0:T(8,128)(2,1)S(1)} fusion(bf16[32,8192]{0,1:T(8,128)(2,1)S(1)} %bitcast.163, s32[4096]{0:T(1024)S(1)} %broadcast_clamp_fusion.1), kind=kCustom, calls=%fused_computation.1 | custom fusion | bytes 540672 | tf_op jit(solution)/shard_map/jit(_take)/gather | solution.py:133
  183.6 25.4 %all-gather.2 = f32[8,1,512]{2,1,0:T(1,128)S(1)} all-gather(f32[1,1,512]{2,1,0:T(1,128)S(1)} %bitcast.209), channel_id=2, replica_groups=mesh['shell'=8,'sector'=32] {'shell'}, dimensions={0}, use_global_device_ids=true | all-gather | bytes 18432 | tf_op jit(solution)/shard_map/all_gather | solution.py:14
  209.4 15.7 %all-reduce.32 = (f32[512]{0:T(512)S(1)}, f32[512]{0:T(512)S(1)}, f32[512]{0:T(512)S(1)}) all-reduce(f32[512]{0:T(512)S(1)} %get-tuple-element.265, f32[512]{0:T(512)S(1)} %get-tuple-element.365, f32[512]{0:T(512)S(1)} %get-tuple-element.364), channel_id=1, replica_groups=mesh['shell'=8,'sector'=32] {'shell'}, use_global_device_ids=true, to_apply=%region_8.9 | all-reduce | flops 1536 | bytes 12288 | tf_op jit(solution)/shard_map/psum | solution.py:154
  227.4 21.0 %all-gather.3 = f32[8,1,512]{2,1,0:T(1,128)S(1)} all-gather(f32[1,1,512]{2,1,0:T(1,128)} %bitcast.210), channel_id=3, replica_groups=mesh['shell'=8,'sector'=32] {'shell'}, dimensions={0}, use_global_device_ids=true | all-gather | bytes 18432 | tf_op jit(solution)/shard_map/all_gather | solution.py:14
  254.0 4.0 fusion.57
  257.9 13.2 %scatter_custom_fusion = f32[32,8192]{0,1:T(8,128)} fusion(s32[4096]{0:T(1024)S(1)} %bitcast.205, f32[4096,32]{1,0:T(8,128)} %fusion.57, f32[]{:T(128)} %constant.164.clone.1), kind=kCustom, calls=%fused_computation.45 | custom fusion | bytes 1049088 | tf_op jit(solution)/shard_map/scatter | solution.py:174
  271.1 3.6 copy.154
  274.7 4.3 all-to-all-start.2
  283.0 12.8 %all-to-all-done.2 = f32[32,32,256]{2,0,1:T(8,128)S(1)} async-done(((f32[32,32,256]{2,0,1:T(8,128)}), f32[32,32,256]{2,0,1:T(8,128)S(1)}, u32[]{:S(2)}, u32[]{:S(2)}) %all-to-all-start.2) | async-done | bytes 1048608 | tf_op jit(solution)/shard_map/all_to_all | solution.py:175
  298.7 44.8 %scatter_custom_fusion.1 = f32[32,4096]{0,1:T(8,128)S(1)} fusion(s32[8192]{0:T(1024)} %bitcast.208, f32[8192,32]{1,0:T(8,128)} %copy.156, f32[]{:T(128)} %constant.164.clone.1), kind=kCustom, calls=%fused_computation.58 | custom fusion | flops 262144 | bytes 524800 | tf_op jit(solution)/shard_map/scatter-add | solution.py:186
  344.5 5.8 convolution_bitcast_fusion.2
  354.2 3.6 fusion.54
  362.8 3.0 copy.204
  422.6 18.2 %pad_add_fusion = f32[8,32,10,10,10]{1,4,3,2,0:T(8,128)} fusion(f32[8,32,8,8,8]{1,4,3,2,0:T(8,128)} %bitcast.148, f32[8,32,8,8,8]{1,4,3,2,0:T(8,128)} %bitcast.149, f32[8,32,8,8,8]{1,4,3,2,0:T(8,128)} %bitcast.150, f32[8,32,8,8,8]{1,4,3,2,0:T(8,128)} %bitcast.151, f32[8,32,8,8,8]{1,4,3,2,0:T(8,128)} %bitcast.152, f32[8,32,8,8,8]{1,4,3,2,0:T(8,128)} %bitcast.153, ...), kind=kLoop, calls=%fused_computation.34 | loop fusion | flops 5376000 | bytes 12558336 | tf_op jit(solution)/shard_map/while/body/eval_jaxpr/transpose(jvp())/add_any | solution.py:33
  452.4 5.3 fusion.1
  457.7 27.7 %all-reduce.31 = (f32[32]{0:T(128)S(1)}, f32[32,64]{1,0:T(8,128)S(1)}, f32[64]{0:T(128)S(1)}, f32[64,2]{0,1:T(2,128)S(1)}) all-reduce(f32[32]{0:T(128)S(1)} %get-tuple-element.294, f32[32,64]{1,0:T(8,128)S(1)} %fusion.21, f32[64]{0:T(128)S(1)} %get-tuple-element.368, ...), channel_id=1, replica_groups=mesh['shell'=8,'sector'=32] {'shell'}, use_global_device_ids=true, to_apply=%region_19.20 | all-reduce | flops 2272 | bytes 18176 | tf_op jit(solution)/shard_map/psum | solution.py:201
  485.4 123.8 %all-reduce.30 = (f32[]{:T(128)}, f32[32]{0:T(128)}, f32[32,64]{1,0:T(8,128)}, f32[64]{0:T(128)}, f32[64,2]{0,1:T(2,128)}) all-reduce(f32[]{:T(128)} %get-tuple-element.359, f32[32]{0:T(128)S(1)} %get-tuple-element.287, f32[32,64]{1,0:T(8,128)S(1)} %get-tuple-element.288, ...), channel_id=1, replica_groups=mesh['shell'=8,'sector'=32] {'sector'}, use_global_device_ids=true, to_apply=%region_10.11 | all-reduce | flops 2273 | bytes 18184 | tf_op jit(solution)/shard_map/psum | solution.py:170
  (217 shorter events, 196.8 us)
Async XLA Ops:
  7.2 107.9 %copy-start = (bf16[32,864]{1,0:T(8,128)(2,1)S(1)}, bf16[32,864]{1,0:T(8,128)(2,1)}, u32[]{:S(2)}) copy-start(bf16[32,864]{1,0:T(8,128)(2,1)} %param.16) | copy-start | bytes 165892
  8.6 112.1 %all-to-all-start = ((s32[32,1,256]{2,1,0:T(1,128)}), s32[32,1,256]{2,1,0:T(1,128)S(1)}, u32[]{:S(2)}, u32[]{:S(2)}) async-start(s32[32,1,256]{2,1,0:T(1,128)} %all_to_all.12), calls=%async_computation | async-start | bytes 65536 | tf_op jit(solution)/shard_map/all_to_all | solution.py:119
  40.6 22.6 %copy-start.3 = (bf16[8,32,8,8,8]{1,4,3,2,0:T(8,128)(2,1)S(1)}, bf16[8,32,8,8,8]{1,4,3,2,0:T(8,128)(2,1)}, u32[]{:S(2)}) copy-start(bf16[8,32,8,8,8]{1,4,3,2,0:T(8,128)(2,1)} %get-tuple-element.335) | copy-start | bytes 786436
  58.6 30.3 %copy-start.7 = (bf16[1,8,32,512]{3,2,1,0:T(8,128)(2,1)S(1)}, bf16[1,8,32,512]{3,2,1,0:T(8,128)(2,1)}, u32[]{:S(2)}) copy-start(bf16[1,8,32,512]{3,2,1,0:T(8,128)(2,1)} %param.15) | copy-start | bytes 786436
  64.2 32.3 %copy-start.2 = (bf16[8,32,8,8,8]{1,4,3,2,0:T(8,128)(2,1)S(1)}, bf16[8,32,8,8,8]{1,4,3,2,0:T(8,128)(2,1)}, u32[]{:S(2)}) copy-start(bf16[8,32,8,8,8]{1,4,3,2,0:T(8,128)(2,1)} %get-tuple-element.341) | copy-start | bytes 786436
  89.7 23.9 %copy-start.8 = (bf16[8,1,32,512]{3,2,1,0:T(8,128)(2,1)S(1)}, bf16[8,1,32,512]{3,2,1,0:T(8,128)(2,1)}, u32[]{:S(2)}) copy-start(bf16[8,1,32,512]{3,2,1,0:T(8,128)(2,1)} %copy.147) | copy-start | bytes 786436
  92.0 23.1 %copy-start.22 = (f32[32]{0:T(128)S(1)}, f32[32]{0:T(128)}, u32[]{:S(2)}) copy-start(f32[32]{0:T(128)} %param.17) | copy-start | bytes 388
  97.6 14.6 %copy-start.10 = (bf16[8,1,32,512]{3,2,1,0:T(8,128)(2,1)S(1)}, bf16[8,1,32,512]{3,2,1,0:T(8,128)(2,1)}, u32[]{:S(2)}) copy-start(bf16[8,1,32,512]{3,2,1,0:T(8,128)(2,1)} %copy.145) | copy-start | bytes 786436
  97.6 15.3 %copy-start.9 = (bf16[8,1,32,512]{3,2,1,0:T(8,128)(2,1)S(1)}, bf16[8,1,32,512]{3,2,1,0:T(8,128)(2,1)}, u32[]{:S(2)}) copy-start(bf16[8,1,32,512]{3,2,1,0:T(8,128)(2,1)} %copy.146) | copy-start | bytes 786436
  97.6 16.8 %copy-start.11 = (bf16[8,1,32,512]{3,2,1,0:T(8,128)(2,1)S(1)}, bf16[8,1,32,512]{3,2,1,0:T(8,128)(2,1)}, u32[]{:S(2)}) copy-start(bf16[8,1,32,512]{3,2,1,0:T(8,128)(2,1)} %copy.148) | copy-start | bytes 786436
  121.4 57.7 %copy-start.14 = (bf16[32,64]{1,0:T(8,128)(2,1)S(1)}, bf16[32,64]{1,0:T(8,128)(2,1)}, u32[]{:S(2)}) copy-start(bf16[32,64]{1,0:T(8,128)(2,1)} %param.18) | copy-start | bytes 12292
  121.4 57.7 %copy-start.23 = (f32[64]{0:T(128)S(1)}, f32[64]{0:T(128)}, u32[]{:S(2)}) copy-start(f32[64]{0:T(128)} %param.19) | copy-start | bytes 772
  145.5 34.5 %copy-start.24 = (f32[64,2]{0,1:T(2,128)S(1)}, f32[64,2]{0,1:T(2,128)}, u32[]{:S(2)}) copy-start(f32[64,2]{0,1:T(2,128)} %param.20) | copy-start | bytes 1540
  147.4 18.6 %all-to-all-start.1 = ((bf16[32,32,256]{2,0,1:T(8,128)(2,1)}), bf16[32,32,256]{2,0,1:T(8,128)(2,1)S(1)}, u32[]{:S(2)}, u32[]{:S(2)}) async-start(bf16[32,32,256]{2,0,1:T(8,128)(2,1)} %select_select_fusion), calls=%async_computation.1 | async-start | bytes 1048576 | tf_op jit(solution)/shard_map/all_to_all | solution.py:126
  154.8 54.2 %copy-start.21 = (f32[8]{0:T(128)}, f32[8]{0:T(128)S(1)}, u32[]{:S(2)}) copy-start(f32[8]{0:T(128)S(1)} %add_multiply_fusion.1) | copy-start | bytes 100
  154.8 70.2 %copy-start.16 = (s32[512]{0:T(512)S(1)}, s32[512]{0:T(512)}, u32[]{:S(2)}) copy-start(s32[512]{0:T(512)} %param.25) | copy-start | bytes 6148
  154.8 70.2 %copy-start.18 = (f32[512]{0:T(512)S(1)}, f32[512]{0:T(512)}, u32[]{:S(2)}) copy-start(f32[512]{0:T(512)} %param.24) | copy-start | bytes 6148
  154.8 70.2 %copy-start.19 = (f32[512]{0:T(512)S(1)}, f32[512]{0:T(512)}, u32[]{:S(2)}) copy-start(f32[512]{0:T(512)} %param.23) | copy-start | bytes 6148
  180.0 74.0 %copy-start.6 = (f32[64,4096]{1,0:T(8,128)}, f32[64,4096]{1,0:T(8,128)S(1)}, u32[]{:S(2)}) copy-start(f32[64,4096]{1,0:T(8,128)S(1)} %fusion) | copy-start | bytes 3145732
  274.7 21.1 %all-to-all-start.2 = ((f32[32,32,256]{2,0,1:T(8,128)}), f32[32,32,256]{2,0,1:T(8,128)S(1)}, u32[]{:S(2)}, u32[]{:S(2)}) async-start(f32[32,32,256]{2,0,1:T(8,128)} %copy.154), calls=%async_computation.2 | async-start | bytes 2097152 | tf_op jit(solution)/shard_map/all_to_all | solution.py:175
  279.0 173.4 %all-reduce.36.cloned.1.call-start = ((), (), s32[]{:S(2)}) async-start(), calls=%async_computation.3 | async-start | bytes 229376 | tf_op jit(solution)/shard_map/psum | solution.py:201
  283.0 61.0 %copy-start.5 = (f32[32,8,512]{2,0,1:T(8,128)S(1)}, f32[32,8,512]{2,0,1:T(8,128)}, u32[]{:S(2)}) copy-start(f32[32,8,512]{2,0,1:T(8,128)} %get-tuple-element.367) | copy-start | bytes 1572868
  357.8 253.1 %all-reduce.38.cloned.1.call-start = ((), (), s32[]{:S(2)}) async-start(), calls=%async_computation.4 | async-start | bytes 229376 | tf_op jit(solution)/shard_map/psum | solution.py:201
  452.4 160.1 %copy-start.1 = (bf16[32,864]{1,0:T(8,128)(2,1)S(1)}, bf16[32,864]{1,0:T(8,128)(2,1)}, u32[]{:S(2)}) copy-start(bf16[32,864]{1,0:T(8,128)(2,1)} %param.16) | copy-start | bytes 165892
  (6 other events, 37.8 us)
Sparse Core Ops, SparseCore 0:
  357.9 67.7 all-reduce.35
  452.5 104.9 all-reduce.37
